TPU v7x, 32 devices: a whole 2x2x4 slice. The times are simulated.
32 devices in a mesh: group: 2 (over y), section: 4 (over z), tensor: 4 (over x, core).
Axes of the slice: x: 2, y: 2, z: 4, core: 2. Of those that a mesh axis runs over, the one named last changes fastest.
Arguments:
- inputs: bfloat16 [48, 4096], P('group', 'tensor'), parts along dimension 0, may hold values from -6 to 6
- gains: float32 [4, 4096], P('section'), may hold values from 0.5 to 1.5
- w_query: bfloat16 [4, 4096, 4096], P('section', None, 'tensor'), may hold values from -0.09375 to 0.09375
- w_key: bfloat16 [4, 4096, 1024], P('section', None, 'tensor'), may hold values from -0.09375 to 0.09375
- w_value: bfloat16 [4, 4096, 1024], P('section', None, 'tensor'), may hold values from -0.09375 to 0.09375
- w_out: bfloat16 [4, 4096, 4096], P('section', 'tensor'), may hold values from -0.375 to 0.375
- key_cache: bfloat16 [4, 48, 128, 1024], P('section', 'group', None, 'tensor'), parts along dimension 1, may hold values from -64 to 64
- value_cache: bfloat16 [4, 48, 128, 1024], P('section', 'group', None, 'tensor'), parts along dimension 1, may hold values from -6 to 6
- cache_lens: int32 [48], P('group'), parts along dimension 0, may hold values from 1 to 128, as said below
- exit_plan: int32 [48], P('group'), parts along dimension 0, may hold values from 1 to 4, as said below
Outputs:
- section_hidden: bfloat16 [4, 48, 4096], P('section', 'group', 'tensor'), parts along dimension 1
- new_keys: bfloat16 [4, 48, 1024], P('section', 'group', 'tensor'), parts along dimension 1
- new_values: bfloat16 [4, 48, 1024], P('section', 'group', 'tensor'), parts along dimension 1
There are 2 independent parts, one for each index of `group`. A program takes and returns all parts, laid end to end along the dimension named above; an argument that names none is the same for every part. Nothing has to cross between parts.
Inputs may be any that keep to these rules, and one draw needn't show every extreme that they name: Cached slots 0 to cache_lens - 1 of a row are live; some row has exactly 128. `exit_plan`: some row runs all 4 layers in full.
All inputs are finite; a program needn't handle non-finite values.
Results may differ from a plain program's by a relative error of at most 0.022.
The roundings to bfloat16 on the way count: a program that leaves them out, or rounds other values in their place, can miss the bound.
Values may be sent and summed in bfloat16 or wider, within the bound.
A program may use at most 128 MiB of HBM per device.

v0:
```python
import math
import jax
import jax.numpy as jnp
from jax import lax
from jax.sharding import PartitionSpec as P

HEAD_DIM = 128
NORM_EPSILON = 1e-05
ROPE_BASE = 500000.0
MASKED_SCORE = -1e30


def shifted(value, axis, steps):
    count = lax.axis_size(axis)
    leading, last = (max(0, -steps), min(count, count - steps))
    return lax.ppermute(value, axis, [(source, source + steps) for source in range(leading, last)])


def rotate(vectors, positions):
    half_dim = vectors.shape[-1] // 2
    frequency = ROPE_BASE ** (-(jnp.arange(half_dim, dtype=jnp.float32) * 2.0 / vectors.shape[-1]))
    angles = positions.astype(jnp.float32)[:, None, None] * frequency[None, None, :]
    cos_part = jnp.cos(angles)
    sin_part = jnp.sin(angles)
    lower_half = vectors[..., :half_dim]
    upper_half = vectors[..., half_dim:]
    return jnp.concatenate(
        [
            lower_half * cos_part - upper_half * sin_part,
            upper_half * cos_part + lower_half * sin_part,
        ],
        axis=-1,
    )


def attend(
    normed, lengths, query_weight, key_weight, value_weight, keys_cached, values_cached, kv_local
):
    row_count = normed.shape[0]
    cache_slots = keys_cached.shape[1]
    per_kv = query_weight.shape[1] // (kv_local * HEAD_DIM)
    inv_root = 1.0 / math.sqrt(HEAD_DIM)
    queries = jnp.dot(normed, query_weight, preferred_element_type=jnp.float32).reshape(
        row_count, kv_local * per_kv, HEAD_DIM
    )
    queries = (
        rotate(queries, lengths).astype(jnp.bfloat16).reshape(row_count, kv_local, per_kv, HEAD_DIM)
    )
    key_new = jnp.dot(normed, key_weight, preferred_element_type=jnp.float32).reshape(
        row_count, kv_local, HEAD_DIM
    )
    key_new = rotate(key_new, lengths).astype(jnp.bfloat16)
    value_new = (
        jnp.dot(normed, value_weight, preferred_element_type=jnp.float32)
        .astype(jnp.bfloat16)
        .reshape(row_count, kv_local, HEAD_DIM)
    )
    keys_old = keys_cached.reshape(row_count, cache_slots, kv_local, HEAD_DIM)
    values_old = values_cached.reshape(row_count, cache_slots, kv_local, HEAD_DIM)
    visible = jnp.arange(cache_slots)[None, :] < lengths[:, None]
    scores_old = (
        jnp.einsum("rhgd,rlhd->rhgl", queries, keys_old, preferred_element_type=jnp.float32)
        * inv_root
    )
    scores_old = jnp.where(visible[:, None, None, :], scores_old, MASKED_SCORE)
    score_new = (
        jnp.einsum("rhgd,rhd->rhg", queries, key_new, preferred_element_type=jnp.float32) * inv_root
    )
    highest = jnp.maximum(jnp.max(scores_old, axis=-1), score_new)
    weight_old = jnp.exp(scores_old - highest[..., None])
    weight_new = jnp.exp(score_new - highest)
    denominator = jnp.sum(weight_old, axis=-1) + weight_new
    weight_old = (weight_old / denominator[..., None]).astype(jnp.bfloat16)
    weight_new = (weight_new / denominator).astype(jnp.bfloat16)
    attended = jnp.einsum(
        "rhgl,rlhd->rhgd", weight_old, values_old, preferred_element_type=jnp.float32
    )
    attended = (
        attended
        + weight_new.astype(jnp.float32)[..., None] * value_new.astype(jnp.float32)[:, :, None, :]
    )
    attended = attended.astype(jnp.bfloat16).reshape(row_count, kv_local * per_kv * HEAD_DIM)
    return (
        attended,
        key_new.reshape(row_count, kv_local * HEAD_DIM),
        value_new.reshape(row_count, kv_local * HEAD_DIM),
    )


def per_device(
    inputs, gains, w_query, w_key, w_value, w_out, key_cache, value_cache, cache_lens, exit_plan
):
    section_count = lax.axis_size("section")
    section_here = lax.axis_index("section")
    tensor_here = lax.axis_index("tensor")
    row_total = inputs.shape[0]
    shard_width = inputs.shape[1]
    kv_local = w_key.shape[2] // HEAD_DIM
    micro_count = 1
    block_rows = row_total // micro_count
    tick_count = section_count + micro_count - 1
    gain_row = gains[0]
    entering_all = lax.all_gather(inputs, "tensor", axis=1, tiled=True)
    carry_width = entering_all.shape[1]

    def advance(step_at, state_now):
        received, out_hidden, out_keys, out_values = state_now
        micro_at = step_at - section_here
        active = jnp.logical_and(micro_at >= 0, micro_at < micro_count)
        current = jnp.where(section_here == 0, entering_all, received)
        running = (section_here < exit_plan).astype(jnp.float32)[:, None]
        widened = current.astype(jnp.float32)
        normed = (
            widened
            * lax.rsqrt(jnp.mean(widened * widened, axis=-1, keepdims=True) + NORM_EPSILON)
            * gain_row[None, :]
        ).astype(jnp.bfloat16)
        keys_cached = key_cache[0]
        values_cached = value_cache[0]
        attended, key_new, value_new = attend(
            normed,
            cache_lens,
            w_query[0],
            w_key[0],
            w_value[0],
            keys_cached,
            values_cached,
            kv_local,
        )
        partial_value = jnp.dot(attended, w_out[0], preferred_element_type=jnp.float32)
        summed = lax.psum(partial_value, "tensor")
        following = (widened + running * summed).astype(jnp.bfloat16)
        own_piece = lax.dynamic_slice_in_dim(following, tensor_here * shard_width, shard_width, 1)
        passed = shifted(following, "section", 1)
        out_hidden = jnp.where(active, own_piece, out_hidden)
        out_keys = jnp.where(active, key_new, out_keys)
        out_values = jnp.where(active, value_new, out_values)
        return (passed, out_hidden, out_keys, out_values)

    initial = (
        jnp.zeros((block_rows, carry_width), jnp.bfloat16),
        jnp.zeros((row_total, shard_width), jnp.bfloat16),
        jnp.zeros((row_total, kv_local * HEAD_DIM), jnp.bfloat16),
        jnp.zeros((row_total, kv_local * HEAD_DIM), jnp.bfloat16),
    )
    final_state = lax.fori_loop(0, tick_count, advance, initial)
    return (final_state[1][None], final_state[2][None], final_state[3][None])


def solution(mesh):
    return jax.shard_map(
        per_device,
        mesh=mesh,
        in_specs=(
            P("group", "tensor"),
            P("section", None),
            P("section", None, "tensor"),
            P("section", None, "tensor"),
            P("section", None, "tensor"),
            P("section", "tensor", None),
            P("section", "group", None, "tensor"),
            P("section", "group", None, "tensor"),
            P("group"),
            P("group"),
        ),
        out_specs=(
            P("section", "group", "tensor"),
            P("section", "group", "tensor"),
            P("section", "group", "tensor"),
        ),
        check_vma=False,
    )
```

profile of v0, /device:TPU:0, one launch (start us, length us, event | category | flops | bytes accessed | tf_op | source)
XLA Modules:
  0.0 274.7 jit_solution(9247631473398930788)
XLA Ops:
  8.0 7.0 %all_gather.3 = bf16[24,4096]{1,0:T(8,128)(2,1)S(1)} all-gather(bf16[24,1024]{1,0:T(8,128)(2,1)} %param.12), channel_id=1, replica_groups=mesh['group'=2,'section'=4,'tensor'=4] {'tensor'}, dimensions={1}, use_global_device_ids=true | all-gather | bytes 245760 | tf_op jit(solution)/shard_map/all_gather | solution.py:103
  15.0 3.5 %squeeze.67 = bf16[24,128,2,128]{3,2,1,0:T(2,128)(2,1)} reshape(bf16[1,24,128,256]{3,2,1,0:T(8,128)(2,1)} %param.18) | data formatting | bytes 3145728 | tf_op jit(solution)/shard_map/while/body/eval_jaxpr/reshape;while/body/eval_jaxpr/squeeze | solution.py:58
  18.5 1.9 squeeze.66
  20.4 2.9 %copy.25 = bf16[1,4096,256]{1,2,0:T(8,128)(2,1)S(1)} copy(bf16[1,4096,256]{2,1,0:T(8,128)(2,1)} %param.15) | data formatting | bytes 4194304
  23.3 11.4 %copy.24 = bf16[1,4096,1024]{1,2,0:T(8,128)(2,1)} copy(bf16[1,4096,1024]{2,1,0:T(8,128)(2,1)} %param.14) | data formatting | bytes 16777216
  34.7 232.8 %while.23 = (s32[]{:T(128)}, bf16[24,4096]{1,0:T(8,128)(2,1)S(1)}, bf16[24,1024]{1,0:T(8,128)(2,1)S(1)}, bf16[24,256]{1,0:T(8,128)(2,1)S(1)}, bf16[24,256]{1,0:T...) while((s32[]{:T(128)}, bf16[24,4096]{1,0:T(8,128)(2,1)S(1)}, ...), condition=%wide.wide.region_5.6_spmd.clone, body=%wide.wide.region_0.5_spmd.clone.sunk | while | flops 518737920 | bytes 52014272 | solution.py:146
  37.2 5.8 %fusion.98 = f32[24,8,128]{2,0,1:T(8,128)S(1)} fusion(bf16[8,128,4096]{2,1,0:T(8,128)(2,1)} %bitcast.101, bf16[24,4096]{1,0:T(8,128)(2,1)S(1)} %get-tuple-element.801, f32[4096]{0:T(1024)S(1)} %bitcast.107, f32[24]{0:T(128)S(1)} %add_rsqrt_fusion.3), kind=kOutput, calls=%fused_computation.22.clone.clone.1 | convolution fusion | flops 201719808 | bytes 8700000 | tf_op jit(solution)/shard_map/while/body/eval_jaxpr/dot_general | solution.py:43
  45.7 5.3 %fusion.106 = f32[24,4096]{1,0:T(8,128)} fusion(bf16[24,1024]{1,0:T(8,128)(2,1)S(1)} %reshape.213, bf16[1,1024,4096]{2,1,0:T(8,128)(2,1)} %get-tuple-element.878), kind=kOutput, calls=%fused_computation.clone.clone.1 | convolution fusion | flops 201326592 | bytes 8830976 | tf_op jit(solution)/shard_map/while/body/eval_jaxpr/dot_general | solution.py:130
  51.2 34.2 %all-reduce.2.cloned.1.call-done = f32[24,4096]{1,0:T(8,128)} async-done(((f32[24,4096]{1,0:T(8,128)}), f32[24,4096]{1,0:T(8,128)}) %all-reduce.2.cloned.1.call-update) | async-done | bytes 393232 | tf_op jit(solution)/shard_map/while/body/eval_jaxpr/psum | solution.py:131
  85.3 1.1 fusion.107
  86.5 3.4 %collective-permute-start = (bf16[24,4096]{1,0:T(8,128)(2,1)S(1)}, bf16[24,4096]{1,0:T(8,128)(2,1)S(1)}, u32[]{:S(2)}, u32[]{:S(2)}) collective-permute-start(bf16[24,4096]{1,0:T(8,128)(2,1)S(1)} %fusion.107), channel_id=1, source_target_pairs={{0,4},{4,8},{8,12},{1,5},{5,9},{9,13},{2,6},{6,10},{10,14},{3,7},{... | collective-permute-start | bytes 589832 | tf_op jit(solution)/shard_map/while/body/eval_jaxpr/ppermute | solution.py:16
  89.9 3.1 %collective-permute-done = bf16[24,4096]{1,0:T(8,128)(2,1)S(1)} collective-permute-done((bf16[24,4096]{1,0:T(8,128)(2,1)S(1)}, bf16[24,4096]{1,0:T(8,128)(2,1)S(1)}, u32[]{:S(2)}, u32[]{:S(2)}) %collective-permute-start) | collective-permute-done | bytes 196640 | tf_op jit(solution)/shard_map/while/body/eval_jaxpr/ppermute | solution.py:16
  95.4 5.8 %fusion.98 = f32[24,8,128]{2,0,1:T(8,128)S(1)} fusion(bf16[8,128,4096]{2,1,0:T(8,128)(2,1)} %bitcast.101, bf16[24,4096]{1,0:T(8,128)(2,1)S(1)} %get-tuple-element.801, f32[4096]{0:T(1024)S(1)} %bitcast.107, f32[24]{0:T(128)S(1)} %add_rsqrt_fusion.3), kind=kOutput, calls=%fused_computation.22.clone.clone.1 | convolution fusion | flops 201719808 | bytes 8700000 | tf_op jit(solution)/shard_map/while/body/eval_jaxpr/dot_general | solution.py:43
  101.9 1.1 fusion.99
  103.9 5.3 %fusion.106 = f32[24,4096]{1,0:T(8,128)} fusion(bf16[24,1024]{1,0:T(8,128)(2,1)S(1)} %reshape.213, bf16[1,1024,4096]{2,1,0:T(8,128)(2,1)} %get-tuple-element.878), kind=kOutput, calls=%fused_computation.clone.clone.1 | convolution fusion | flops 201326592 | bytes 8830976 | tf_op jit(solution)/shard_map/while/body/eval_jaxpr/dot_general | solution.py:130
  109.4 34.1 %all-reduce.2.cloned.1.call-done = f32[24,4096]{1,0:T(8,128)} async-done(((f32[24,4096]{1,0:T(8,128)}), f32[24,4096]{1,0:T(8,128)}) %all-reduce.2.cloned.1.call-update) | async-done | bytes 393232 | tf_op jit(solution)/shard_map/while/body/eval_jaxpr/psum | solution.py:131
  143.5 1.1 fusion.107
  144.6 3.4 %collective-permute-start = (bf16[24,4096]{1,0:T(8,128)(2,1)S(1)}, bf16[24,4096]{1,0:T(8,128)(2,1)S(1)}, u32[]{:S(2)}, u32[]{:S(2)}) collective-permute-start(bf16[24,4096]{1,0:T(8,128)(2,1)S(1)} %fusion.107), channel_id=1, source_target_pairs={{0,4},{4,8},{8,12},{1,5},{5,9},{9,13},{2,6},{6,10},{10,14},{3,7},{... | collective-permute-start | bytes 589832 | tf_op jit(solution)/shard_map/while/body/eval_jaxpr/ppermute | solution.py:16
  148.1 3.1 %collective-permute-done = bf16[24,4096]{1,0:T(8,128)(2,1)S(1)} collective-permute-done((bf16[24,4096]{1,0:T(8,128)(2,1)S(1)}, bf16[24,4096]{1,0:T(8,128)(2,1)S(1)}, u32[]{:S(2)}, u32[]{:S(2)}) %collective-permute-start) | collective-permute-done | bytes 196640 | tf_op jit(solution)/shard_map/while/body/eval_jaxpr/ppermute | solution.py:16
  153.6 5.8 %fusion.98 = f32[24,8,128]{2,0,1:T(8,128)S(1)} fusion(bf16[8,128,4096]{2,1,0:T(8,128)(2,1)} %bitcast.101, bf16[24,4096]{1,0:T(8,128)(2,1)S(1)} %get-tuple-element.801, f32[4096]{0:T(1024)S(1)} %bitcast.107, f32[24]{0:T(128)S(1)} %add_rsqrt_fusion.3), kind=kOutput, calls=%fused_computation.22.clone.clone.1 | convolution fusion | flops 201719808 | bytes 8700000 | tf_op jit(solution)/shard_map/while/body/eval_jaxpr/dot_general | solution.py:43
  162.1 5.3 %fusion.106 = f32[24,4096]{1,0:T(8,128)} fusion(bf16[24,1024]{1,0:T(8,128)(2,1)S(1)} %reshape.213, bf16[1,1024,4096]{2,1,0:T(8,128)(2,1)} %get-tuple-element.878), kind=kOutput, calls=%fused_computation.clone.clone.1 | convolution fusion | flops 201326592 | bytes 8830976 | tf_op jit(solution)/shard_map/while/body/eval_jaxpr/dot_general | solution.py:130
  167.6 34.1 %all-reduce.2.cloned.1.call-done = f32[24,4096]{1,0:T(8,128)} async-done(((f32[24,4096]{1,0:T(8,128)}), f32[24,4096]{1,0:T(8,128)}) %all-reduce.2.cloned.1.call-update) | async-done | bytes 393232 | tf_op jit(solution)/shard_map/while/body/eval_jaxpr/psum | solution.py:131
  201.7 1.1 fusion.107
  202.8 3.4 %collective-permute-start = (bf16[24,4096]{1,0:T(8,128)(2,1)S(1)}, bf16[24,4096]{1,0:T(8,128)(2,1)S(1)}, u32[]{:S(2)}, u32[]{:S(2)}) collective-permute-start(bf16[24,4096]{1,0:T(8,128)(2,1)S(1)} %fusion.107), channel_id=1, source_target_pairs={{0,4},{4,8},{8,12},{1,5},{5,9},{9,13},{2,6},{6,10},{10,14},{3,7},{... | collective-permute-start | bytes 589832 | tf_op jit(solution)/shard_map/while/body/eval_jaxpr/ppermute | solution.py:16
  206.2 3.1 %collective-permute-done = bf16[24,4096]{1,0:T(8,128)(2,1)S(1)} collective-permute-done((bf16[24,4096]{1,0:T(8,128)(2,1)S(1)}, bf16[24,4096]{1,0:T(8,128)(2,1)S(1)}, u32[]{:S(2)}, u32[]{:S(2)}) %collective-permute-start) | collective-permute-done | bytes 196640 | tf_op jit(solution)/shard_map/while/body/eval_jaxpr/ppermute | solution.py:16
  211.7 5.8 %fusion.98 = f32[24,8,128]{2,0,1:T(8,128)S(1)} fusion(bf16[8,128,4096]{2,1,0:T(8,128)(2,1)} %bitcast.101, bf16[24,4096]{1,0:T(8,128)(2,1)S(1)} %get-tuple-element.801, f32[4096]{0:T(1024)S(1)} %bitcast.107, f32[24]{0:T(128)S(1)} %add_rsqrt_fusion.3), kind=kOutput, calls=%fused_computation.22.clone.clone.1 | convolution fusion | flops 201719808 | bytes 8700000 | tf_op jit(solution)/shard_map/while/body/eval_jaxpr/dot_general | solution.py:43
  218.2 1.1 fusion.99
  220.3 5.3 %fusion.106 = f32[24,4096]{1,0:T(8,128)} fusion(bf16[24,1024]{1,0:T(8,128)(2,1)S(1)} %reshape.213, bf16[1,1024,4096]{2,1,0:T(8,128)(2,1)} %get-tuple-element.878), kind=kOutput, calls=%fused_computation.clone.clone.1 | convolution fusion | flops 201326592 | bytes 8830976 | tf_op jit(solution)/shard_map/while/body/eval_jaxpr/dot_general | solution.py:130
  225.7 34.1 %all-reduce.2.cloned.1.call-done = f32[24,4096]{1,0:T(8,128)} async-done(((f32[24,4096]{1,0:T(8,128)}), f32[24,4096]{1,0:T(8,128)}) %all-reduce.2.cloned.1.call-update) | async-done | bytes 393232 | tf_op jit(solution)/shard_map/while/body/eval_jaxpr/psum | solution.py:131
  259.8 1.1 fusion.107
  260.9 3.4 %collective-permute-start = (bf16[24,4096]{1,0:T(8,128)(2,1)S(1)}, bf16[24,4096]{1,0:T(8,128)(2,1)S(1)}, u32[]{:S(2)}, u32[]{:S(2)}) collective-permute-start(bf16[24,4096]{1,0:T(8,128)(2,1)S(1)} %fusion.107), channel_id=1, source_target_pairs={{0,4},{4,8},{8,12},{1,5},{5,9},{9,13},{2,6},{6,10},{10,14},{3,7},{... | collective-permute-start | bytes 589832 | tf_op jit(solution)/shard_map/while/body/eval_jaxpr/ppermute | solution.py:16
  264.4 3.1 %collective-permute-done = bf16[24,4096]{1,0:T(8,128)(2,1)S(1)} collective-permute-done((bf16[24,4096]{1,0:T(8,128)(2,1)S(1)}, bf16[24,4096]{1,0:T(8,128)(2,1)S(1)}, u32[]{:S(2)}, u32[]{:S(2)}) %collective-permute-start) | collective-permute-done | bytes 196640 | tf_op jit(solution)/shard_map/while/body/eval_jaxpr/ppermute | solution.py:16
  (141 shorter events, 20.0 us)
Async XLA Ops:
  7.2 11.3 %copy-start.2 = (bf16[1,24,128,256]{3,2,1,0:T(8,128)(2,1)S(1)}, bf16[1,24,128,256]{3,2,1,0:T(8,128)(2,1)}, u32[]{:S(2)}) copy-start(bf16[1,24,128,256]{3,2,1,0:T(8,128)(2,1)} %param.19) | copy-start | bytes 4718596
  23.3 11.4 %copy-start.1 = (f32[1,4096]{1,0:T(1,128)S(1)}, f32[1,4096]{1,0:T(1,128)}, u32[]{:S(2)}) copy-start(f32[1,4096]{1,0:T(1,128)} %param.13) | copy-start | bytes 49156
  23.3 11.4 %copy-start.8 = (s32[24]{0:T(128)S(1)}, s32[24]{0:T(128)}, u32[]{:S(2)}) copy-start(s32[24]{0:T(128)} %param.20) | copy-start | bytes 292
  23.3 11.4 %copy-start.9 = (s32[24]{0:T(128)S(1)}, s32[24]{0:T(128)}, u32[]{:S(2)}) copy-start(s32[24]{0:T(128)} %param.21) | copy-start | bytes 292
  34.8 50.6 %all-reduce.2.cloned.1.call-start = ((), (), s32[]{:S(2)}) async-start(), calls=%async_computation | async-start | bytes 786432 | tf_op jit(solution)/shard_map/while/body/eval_jaxpr/psum | solution.py:131
  35.1 1.6 copy-start
  37.2 6.5 %copy-start.3 = (bf16[24,128,2,128]{3,2,1,0:T(2,128)(2,1)S(1)}, bf16[24,128,2,128]{3,2,1,0:T(2,128)(2,1)}, u32[]{:S(2)}) copy-start(bf16[24,128,2,128]{3,2,1,0:T(2,128)(2,1)} %get-tuple-element.881) | copy-start | bytes 4718596 | tf_op jit(solution)/shard_map/while
  43.0 2.1 copy-start.4
  86.5 6.6 %collective-permute-start = (bf16[24,4096]{1,0:T(8,128)(2,1)S(1)}, bf16[24,4096]{1,0:T(8,128)(2,1)S(1)}, u32[]{:S(2)}, u32[]{:S(2)}) collective-permute-start(bf16[24,4096]{1,0:T(8,128)(2,1)S(1)} %fusion.107), channel_id=1, source_target_pairs={{0,4},{4,8},{8,12},{1,5},{5,9},{9,13},{2,6},{6,10},{10,14},{3,7},{... | collective-permute-start | bytes 589832 | tf_op jit(solution)/shard_map/while/body/eval_jaxpr/ppermute | solution.py:16
  93.0 50.5 %all-reduce.2.cloned.1.call-start = ((), (), s32[]{:S(2)}) async-start(), calls=%async_computation | async-start | bytes 786432 | tf_op jit(solution)/shard_map/while/body/eval_jaxpr/psum | solution.py:131
  93.3 1.6 copy-start
  95.4 6.5 %copy-start.3 = (bf16[24,128,2,128]{3,2,1,0:T(2,128)(2,1)S(1)}, bf16[24,128,2,128]{3,2,1,0:T(2,128)(2,1)}, u32[]{:S(2)}) copy-start(bf16[24,128,2,128]{3,2,1,0:T(2,128)(2,1)} %get-tuple-element.881) | copy-start | bytes 4718596 | tf_op jit(solution)/shard_map/while
  101.2 2.1 copy-start.4
  144.6 6.6 %collective-permute-start = (bf16[24,4096]{1,0:T(8,128)(2,1)S(1)}, bf16[24,4096]{1,0:T(8,128)(2,1)S(1)}, u32[]{:S(2)}, u32[]{:S(2)}) collective-permute-start(bf16[24,4096]{1,0:T(8,128)(2,1)S(1)} %fusion.107), channel_id=1, source_target_pairs={{0,4},{4,8},{8,12},{1,5},{5,9},{9,13},{2,6},{6,10},{10,14},{3,7},{... | collective-permute-start | bytes 589832 | tf_op jit(solution)/shard_map/while/body/eval_jaxpr/ppermute | solution.py:16
  151.2 50.5 %all-reduce.2.cloned.1.call-start = ((), (), s32[]{:S(2)}) async-start(), calls=%async_computation | async-start | bytes 786432 | tf_op jit(solution)/shard_map/while/body/eval_jaxpr/psum | solution.py:131
  151.5 1.6 copy-start
  153.6 6.5 %copy-start.3 = (bf16[24,128,2,128]{3,2,1,0:T(2,128)(2,1)S(1)}, bf16[24,128,2,128]{3,2,1,0:T(2,128)(2,1)}, u32[]{:S(2)}) copy-start(bf16[24,128,2,128]{3,2,1,0:T(2,128)(2,1)} %get-tuple-element.881) | copy-start | bytes 4718596 | tf_op jit(solution)/shard_map/while
  159.3 2.1 copy-start.4
  202.8 6.6 %collective-permute-start = (bf16[24,4096]{1,0:T(8,128)(2,1)S(1)}, bf16[24,4096]{1,0:T(8,128)(2,1)S(1)}, u32[]{:S(2)}, u32[]{:S(2)}) collective-permute-start(bf16[24,4096]{1,0:T(8,128)(2,1)S(1)} %fusion.107), channel_id=1, source_target_pairs={{0,4},{4,8},{8,12},{1,5},{5,9},{9,13},{2,6},{6,10},{10,14},{3,7},{... | collective-permute-start | bytes 589832 | tf_op jit(solution)/shard_map/while/body/eval_jaxpr/ppermute | solution.py:16
  209.3 50.5 %all-reduce.2.cloned.1.call-start = ((), (), s32[]{:S(2)}) async-start(), calls=%async_computation | async-start | bytes 786432 | tf_op jit(solution)/shard_map/while/body/eval_jaxpr/psum | solution.py:131
  209.6 1.6 copy-start
  211.7 6.5 %copy-start.3 = (bf16[24,128,2,128]{3,2,1,0:T(2,128)(2,1)S(1)}, bf16[24,128,2,128]{3,2,1,0:T(2,128)(2,1)}, u32[]{:S(2)}) copy-start(bf16[24,128,2,128]{3,2,1,0:T(2,128)(2,1)} %get-tuple-element.881) | copy-start | bytes 4718596 | tf_op jit(solution)/shard_map/while
  217.5 2.1 copy-start.4
  260.9 6.6 %collective-permute-start = (bf16[24,4096]{1,0:T(8,128)(2,1)S(1)}, bf16[24,4096]{1,0:T(8,128)(2,1)S(1)}, u32[]{:S(2)}, u32[]{:S(2)}) collective-permute-start(bf16[24,4096]{1,0:T(8,128)(2,1)S(1)} %fusion.107), channel_id=1, source_target_pairs={{0,4},{4,8},{8,12},{1,5},{5,9},{9,13},{2,6},{6,10},{10,14},{3,7},{... | collective-permute-start | bytes 589832 | tf_op jit(solution)/shard_map/while/body/eval_jaxpr/ppermute | solution.py:16
  267.5 0.6 copy-start.5
  267.5 0.6 copy-start.6
  267.5 0.6 copy-start.7
Sparse Core Ops, SparseCore 0:
  51.2 34.0 all-reduce.1
  109.4 34.0 all-reduce.1
  167.6 34.0 all-reduce.1
  225.8 34.0 all-reduce.1
where the time goes:
time: 276 us; the launch traced here: 275 us
  waiting for transfers between devices  149 us (54%)
  matrix products  56.4 us (20%)
  local copies, waits for them, and re-layouts  24.5 us (9%)
  between operations  13.8 us (5%)
  starting transfers between devices  13.7 us (5%)
  other arithmetic  9.68 us (4%)
  blocking collectives  7.03 us (3%)
    psum x4, waiting for transfers between devices, advance(): summed = lax.psum(partial_value, 'tensor')  136 us
    dot_general x4, matrix products, attend(): jnp.dot(normed, query_weight, preferred_element_type=jnp.float32)  23.1 us
    dot_general x4, matrix products, advance(): jnp.dot(attended, w_out[0], preferred_element_type=jnp.float32)  21.3 us
    unnamed x16, local copies, waits for them, and re-layouts  14.9 us
    ppermute x4, starting transfers between devices, shifted(): lax.ppermute(value, axis, [(source, source + steps) for source in range(l...  13.6 us
    ppermute x4, waiting for transfers between devices, shifted(): lax.ppermute(value, axis, [(source, source + steps) for source in range(l...  12.5 us
    all_gather x1, blocking collectives, per_device(): entering_all = lax.all_gather(inputs, 'tensor', axis=1, tiled=True)  7.03 us
  transfers between devices with their start and end apart: 8, of which 8 were waited for; matrix products, arithmetic and copies ran while one was open for 0% of the time, Pallas kernels for 0%

commit v1 on v0

--- a/solution.py
+++ b/solution.py
@@ -128,7 +128,7 @@
             kv_local,
         )
         partial_value = jnp.dot(attended, w_out[0], preferred_element_type=jnp.float32)
-        summed = lax.psum(partial_value, "tensor")
+        summed = jnp.sum(lax.all_gather(partial_value, "tensor"), axis=0)
         following = (widened + running * summed).astype(jnp.bfloat16)
         own_piece = lax.dynamic_slice_in_dim(following, tensor_here * shard_width, shard_width, 1)
         passed = shifted(following, "section", 1)

time: 276 us -> 230 us (0.83)
  waiting for transfers between devices: 149 us -> 101 us
    psum x4 -> x0, waiting for transfers between devices: 136 us -> none  [advance(): summed = lax.psum(partial_value, 'tensor')]
    all_gather x0 -> x4, waiting for transfers between devices: none -> 83.4 us  [advance(): summed = jnp.sum(lax.all_gather(partial_value, 'tensor'), axis=0)]
    reduce_sum x0 -> x4, other arithmetic: none -> 6.13 us  [advance(): summed = jnp.sum(lax.all_gather(partial_value, 'tensor'), axis=0)]
    ppermute x4, waiting for transfers between devices: 12.5 us -> 18 us  [shifted(): lax.ppermute(value, axis, [(source, source + steps) for source in range(l...]
    convert_element_type x4, other arithmetic: 4.44 us -> 0.47 us  [advance(): following = (widened + running * summed).astype(jnp.bfloat16)]
where the time goes in v1:
time: 230 us; the launch traced here: 229 us
  waiting for transfers between devices  101 us (44%)
  matrix products  56.5 us (25%)
  local copies, waits for them, and re-layouts  24.5 us (11%)
  between operations  13.8 us (6%)
  starting transfers between devices  13.7 us (6%)
  other arithmetic  11.8 us (5%)
  blocking collectives  7.03 us (3%)
    all_gather x4, waiting for transfers between devices, advance(): summed = jnp.sum(lax.all_gather(partial_value, 'tensor'), axis=0)  83.4 us
    dot_general x4, matrix products, attend(): jnp.dot(normed, query_weight, preferred_element_type=jnp.float32)  23.1 us
    dot_general x4, matrix products, advance(): jnp.dot(attended, w_out[0], preferred_element_type=jnp.float32)  21.5 us
    ppermute x4, waiting for transfers between devices, shifted(): lax.ppermute(value, axis, [(source, source + steps) for source in range(l...  18 us
    unnamed x16, local copies, waits for them, and re-layouts  14.9 us
    ppermute x4, starting transfers between devices, shifted(): lax.ppermute(value, axis, [(source, source + steps) for source in range(l...  13.6 us
    all_gather x1, blocking collectives, per_device(): entering_all = lax.all_gather(inputs, 'tensor', axis=1, tiled=True)  7.03 us
    reduce_sum x4, other arithmetic, advance(): summed = jnp.sum(lax.all_gather(partial_value, 'tensor'), axis=0)  6.13 us
  transfers between devices with their start and end apart: 8, of which 8 were waited for; matrix products, arithmetic and copies ran while one was open for 0% of the time, Pallas kernels for 0%

profile of v1, /device:TPU:0, one launch (start us, length us, event | category | flops | bytes accessed | tf_op | source)
XLA Modules:
  0.0 229.4 jit_solution(15585385983247868905)
XLA Ops:
  8.0 7.0 %all_gather.23 = bf16[24,4096]{1,0:T(8,128)(2,1)S(1)} all-gather(bf16[24,1024]{1,0:T(8,128)(2,1)} %param.12), channel_id=1, replica_groups=mesh['group'=2,'section'=4,'tensor'=4] {'tensor'}, dimensions={1}, use_global_device_ids=true | all-gather | bytes 245760 | tf_op jit(solution)/shard_map/all_gather | solution.py:103
  15.0 3.5 %squeeze.67 = bf16[24,128,2,128]{3,2,1,0:T(2,128)(2,1)} reshape(bf16[1,24,128,256]{3,2,1,0:T(8,128)(2,1)} %param.18) | data formatting | bytes 3145728 | tf_op jit(solution)/shard_map/while/body/eval_jaxpr/reshape;while/body/eval_jaxpr/squeeze | solution.py:58
  18.5 1.9 squeeze.66
  20.4 2.9 %copy.25 = bf16[1,4096,256]{1,2,0:T(8,128)(2,1)S(1)} copy(bf16[1,4096,256]{2,1,0:T(8,128)(2,1)} %param.15) | data formatting | bytes 4194304
  23.3 11.4 %copy.24 = bf16[1,4096,1024]{1,2,0:T(8,128)(2,1)} copy(bf16[1,4096,1024]{2,1,0:T(8,128)(2,1)} %param.14) | data formatting | bytes 16777216
  34.8 187.5 %while.23 = (s32[]{:T(128)}, bf16[24,4096]{1,0:T(8,128)(2,1)S(1)}, bf16[24,1024]{1,0:T(8,128)(2,1)S(1)}, bf16[24,256]{1,0:T(8,128)(2,1)S(1)}, bf16[24,256]{1,0:T...) while((s32[]{:T(128)}, bf16[24,4096]{1,0:T(8,128)(2,1)S(1)}, ...), condition=%wide.wide.region_5.6_spmd.clone, body=%wide.wide.region_0.5_spmd.clone.sunk | while | flops 518934528 | bytes 57519312 | solution.py:146
  37.2 5.8 %fusion.98 = f32[24,8,128]{2,0,1:T(8,128)S(1)} fusion(bf16[8,128,4096]{2,1,0:T(8,128)(2,1)} %bitcast.105, bf16[24,4096]{1,0:T(8,128)(2,1)S(1)} %get-tuple-element.801, f32[4096]{0:T(1024)S(1)} %bitcast.112, f32[24]{0:T(128)S(1)} %add_rsqrt_fusion.3), kind=kOutput, calls=%fused_computation.22.clone.clone.1 | convolution fusion | flops 201719808 | bytes 8700000 | tf_op jit(solution)/shard_map/while/body/eval_jaxpr/dot_general | solution.py:43
  43.7 1.1 fusion.99
  45.7 5.4 %fusion.106 = f32[24,4096]{1,0:T(8,128)} fusion(bf16[24,1024]{1,0:T(8,128)(2,1)S(1)} %reshape.215, bf16[1,1024,4096]{2,1,0:T(8,128)(2,1)} %get-tuple-element.880), kind=kOutput, calls=%fused_computation.clone.clone.1 | convolution fusion | flops 201326592 | bytes 8830976 | tf_op jit(solution)/shard_map/while/body/eval_jaxpr/dot_general | solution.py:130
  51.2 21.2 %all-gather.7.cloned.1.call-done = f32[96,4096]{1,0:T(8,128)} async-done(((f32[24,4096]{1,0:T(8,128)}), f32[96,4096]{1,0:T(8,128)}) %all-gather.7.cloned.1.call-update) | async-done | bytes 1572880 | tf_op jit(solution)/shard_map/while/body/eval_jaxpr/all_gather | solution.py:131
  72.4 1.5 reduce_sum.61
  74.1 3.4 %collective-permute-start = (bf16[24,4096]{1,0:T(8,128)(2,1)S(1)}, bf16[24,4096]{1,0:T(8,128)(2,1)S(1)}, u32[]{:S(2)}, u32[]{:S(2)}) collective-permute-start(bf16[24,4096]{1,0:T(8,128)(2,1)S(1)} %fusion.107), channel_id=1, source_target_pairs={{0,4},{4,8},{8,12},{1,5},{5,9},{9,13},{2,6},{6,10},{10,14},{3,7},{... | collective-permute-start | bytes 589832 | tf_op jit(solution)/shard_map/while/body/eval_jaxpr/ppermute | solution.py:16
  77.5 4.5 %collective-permute-done = bf16[24,4096]{1,0:T(8,128)(2,1)S(1)} collective-permute-done((bf16[24,4096]{1,0:T(8,128)(2,1)S(1)}, bf16[24,4096]{1,0:T(8,128)(2,1)S(1)}, u32[]{:S(2)}, u32[]{:S(2)}) %collective-permute-start) | collective-permute-done | bytes 196640 | tf_op jit(solution)/shard_map/while/body/eval_jaxpr/ppermute | solution.py:16
  84.4 5.8 %fusion.98 = f32[24,8,128]{2,0,1:T(8,128)S(1)} fusion(bf16[8,128,4096]{2,1,0:T(8,128)(2,1)} %bitcast.105, bf16[24,4096]{1,0:T(8,128)(2,1)S(1)} %get-tuple-element.801, f32[4096]{0:T(1024)S(1)} %bitcast.112, f32[24]{0:T(128)S(1)} %add_rsqrt_fusion.3), kind=kOutput, calls=%fused_computation.22.clone.clone.1 | convolution fusion | flops 201719808 | bytes 8700000 | tf_op jit(solution)/shard_map/while/body/eval_jaxpr/dot_general | solution.py:43
  90.9 1.1 fusion.99
  93.0 5.4 %fusion.106 = f32[24,4096]{1,0:T(8,128)} fusion(bf16[24,1024]{1,0:T(8,128)(2,1)S(1)} %reshape.215, bf16[1,1024,4096]{2,1,0:T(8,128)(2,1)} %get-tuple-element.880), kind=kOutput, calls=%fused_computation.clone.clone.1 | convolution fusion | flops 201326592 | bytes 8830976 | tf_op jit(solution)/shard_map/while/body/eval_jaxpr/dot_general | solution.py:130
  98.5 20.7 %all-gather.7.cloned.1.call-done = f32[96,4096]{1,0:T(8,128)} async-done(((f32[24,4096]{1,0:T(8,128)}), f32[96,4096]{1,0:T(8,128)}) %all-gather.7.cloned.1.call-update) | async-done | bytes 1572880 | tf_op jit(solution)/shard_map/while/body/eval_jaxpr/all_gather | solution.py:131
  119.2 1.5 reduce_sum.61
  120.8 3.4 %collective-permute-start = (bf16[24,4096]{1,0:T(8,128)(2,1)S(1)}, bf16[24,4096]{1,0:T(8,128)(2,1)S(1)}, u32[]{:S(2)}, u32[]{:S(2)}) collective-permute-start(bf16[24,4096]{1,0:T(8,128)(2,1)S(1)} %fusion.107), channel_id=1, source_target_pairs={{0,4},{4,8},{8,12},{1,5},{5,9},{9,13},{2,6},{6,10},{10,14},{3,7},{... | collective-permute-start | bytes 589832 | tf_op jit(solution)/shard_map/while/body/eval_jaxpr/ppermute | solution.py:16
  124.3 4.5 %collective-permute-done = bf16[24,4096]{1,0:T(8,128)(2,1)S(1)} collective-permute-done((bf16[24,4096]{1,0:T(8,128)(2,1)S(1)}, bf16[24,4096]{1,0:T(8,128)(2,1)S(1)}, u32[]{:S(2)}, u32[]{:S(2)}) %collective-permute-start) | collective-permute-done | bytes 196640 | tf_op jit(solution)/shard_map/while/body/eval_jaxpr/ppermute | solution.py:16
  131.1 5.8 %fusion.98 = f32[24,8,128]{2,0,1:T(8,128)S(1)} fusion(bf16[8,128,4096]{2,1,0:T(8,128)(2,1)} %bitcast.105, bf16[24,4096]{1,0:T(8,128)(2,1)S(1)} %get-tuple-element.801, f32[4096]{0:T(1024)S(1)} %bitcast.112, f32[24]{0:T(128)S(1)} %add_rsqrt_fusion.3), kind=kOutput, calls=%fused_computation.22.clone.clone.1 | convolution fusion | flops 201719808 | bytes 8700000 | tf_op jit(solution)/shard_map/while/body/eval_jaxpr/dot_general | solution.py:43
  139.7 5.4 %fusion.106 = f32[24,4096]{1,0:T(8,128)} fusion(bf16[24,1024]{1,0:T(8,128)(2,1)S(1)} %reshape.215, bf16[1,1024,4096]{2,1,0:T(8,128)(2,1)} %get-tuple-element.880), kind=kOutput, calls=%fused_computation.clone.clone.1 | convolution fusion | flops 201326592 | bytes 8830976 | tf_op jit(solution)/shard_map/while/body/eval_jaxpr/dot_general | solution.py:130
  145.2 20.7 %all-gather.7.cloned.1.call-done = f32[96,4096]{1,0:T(8,128)} async-done(((f32[24,4096]{1,0:T(8,128)}), f32[96,4096]{1,0:T(8,128)}) %all-gather.7.cloned.1.call-update) | async-done | bytes 1572880 | tf_op jit(solution)/shard_map/while/body/eval_jaxpr/all_gather | solution.py:131
  165.9 1.5 reduce_sum.61
  167.6 3.4 %collective-permute-start = (bf16[24,4096]{1,0:T(8,128)(2,1)S(1)}, bf16[24,4096]{1,0:T(8,128)(2,1)S(1)}, u32[]{:S(2)}, u32[]{:S(2)}) collective-permute-start(bf16[24,4096]{1,0:T(8,128)(2,1)S(1)} %fusion.107), channel_id=1, source_target_pairs={{0,4},{4,8},{8,12},{1,5},{5,9},{9,13},{2,6},{6,10},{10,14},{3,7},{... | collective-permute-start | bytes 589832 | tf_op jit(solution)/shard_map/while/body/eval_jaxpr/ppermute | solution.py:16
  171.0 4.5 %collective-permute-done = bf16[24,4096]{1,0:T(8,128)(2,1)S(1)} collective-permute-done((bf16[24,4096]{1,0:T(8,128)(2,1)S(1)}, bf16[24,4096]{1,0:T(8,128)(2,1)S(1)}, u32[]{:S(2)}, u32[]{:S(2)}) %collective-permute-start) | collective-permute-done | bytes 196640 | tf_op jit(solution)/shard_map/while/body/eval_jaxpr/ppermute | solution.py:16
  177.9 5.8 %fusion.98 = f32[24,8,128]{2,0,1:T(8,128)S(1)} fusion(bf16[8,128,4096]{2,1,0:T(8,128)(2,1)} %bitcast.105, bf16[24,4096]{1,0:T(8,128)(2,1)S(1)} %get-tuple-element.801, f32[4096]{0:T(1024)S(1)} %bitcast.112, f32[24]{0:T(128)S(1)} %add_rsqrt_fusion.3), kind=kOutput, calls=%fused_computation.22.clone.clone.1 | convolution fusion | flops 201719808 | bytes 8700000 | tf_op jit(solution)/shard_map/while/body/eval_jaxpr/dot_general | solution.py:43
  186.4 5.4 %fusion.106 = f32[24,4096]{1,0:T(8,128)} fusion(bf16[24,1024]{1,0:T(8,128)(2,1)S(1)} %reshape.215, bf16[1,1024,4096]{2,1,0:T(8,128)(2,1)} %get-tuple-element.880), kind=kOutput, calls=%fused_computation.clone.clone.1 | convolution fusion | flops 201326592 | bytes 8830976 | tf_op jit(solution)/shard_map/while/body/eval_jaxpr/dot_general | solution.py:130
  191.9 20.7 %all-gather.7.cloned.1.call-done = f32[96,4096]{1,0:T(8,128)} async-done(((f32[24,4096]{1,0:T(8,128)}), f32[96,4096]{1,0:T(8,128)}) %all-gather.7.cloned.1.call-update) | async-done | bytes 1572880 | tf_op jit(solution)/shard_map/while/body/eval_jaxpr/all_gather | solution.py:131
  212.6 1.5 reduce_sum.61
  214.3 3.4 %collective-permute-start = (bf16[24,4096]{1,0:T(8,128)(2,1)S(1)}, bf16[24,4096]{1,0:T(8,128)(2,1)S(1)}, u32[]{:S(2)}, u32[]{:S(2)}) collective-permute-start(bf16[24,4096]{1,0:T(8,128)(2,1)S(1)} %fusion.107), channel_id=1, source_target_pairs={{0,4},{4,8},{8,12},{1,5},{5,9},{9,13},{2,6},{6,10},{10,14},{3,7},{... | collective-permute-start | bytes 589832 | tf_op jit(solution)/shard_map/while/body/eval_jaxpr/ppermute | solution.py:16
  217.7 4.5 %collective-permute-done = bf16[24,4096]{1,0:T(8,128)(2,1)S(1)} collective-permute-done((bf16[24,4096]{1,0:T(8,128)(2,1)S(1)}, bf16[24,4096]{1,0:T(8,128)(2,1)S(1)}, u32[]{:S(2)}, u32[]{:S(2)}) %collective-permute-start) | collective-permute-done | bytes 196640 | tf_op jit(solution)/shard_map/while/body/eval_jaxpr/ppermute | solution.py:16
  (145 shorter events, 20.4 us)
Async XLA Ops:
  7.2 11.3 %copy-start.2 = (bf16[1,24,128,256]{3,2,1,0:T(8,128)(2,1)S(1)}, bf16[1,24,128,256]{3,2,1,0:T(8,128)(2,1)}, u32[]{:S(2)}) copy-start(bf16[1,24,128,256]{3,2,1,0:T(8,128)(2,1)} %param.19) | copy-start | bytes 4718596
  23.3 11.4 %copy-start.1 = (f32[1,4096]{1,0:T(1,128)S(1)}, f32[1,4096]{1,0:T(1,128)}, u32[]{:S(2)}) copy-start(f32[1,4096]{1,0:T(1,128)} %param.13) | copy-start | bytes 49156
  23.3 11.4 %copy-start.8 = (s32[24]{0:T(128)S(1)}, s32[24]{0:T(128)}, u32[]{:S(2)}) copy-start(s32[24]{0:T(128)} %param.20) | copy-start | bytes 292
  23.3 11.4 %copy-start.9 = (s32[24]{0:T(128)S(1)}, s32[24]{0:T(128)}, u32[]{:S(2)}) copy-start(s32[24]{0:T(128)} %param.21) | copy-start | bytes 292
  34.8 37.7 %all-gather.7.cloned.1.call-start = ((), (), s32[]{:S(2)}) async-start(), calls=%async_computation | async-start | bytes 1966080 | tf_op jit(solution)/shard_map/while/body/eval_jaxpr/all_gather | solution.py:131
  35.1 1.6 copy-start
  37.2 6.5 %copy-start.3 = (bf16[24,128,2,128]{3,2,1,0:T(2,128)(2,1)S(1)}, bf16[24,128,2,128]{3,2,1,0:T(2,128)(2,1)}, u32[]{:S(2)}) copy-start(bf16[24,128,2,128]{3,2,1,0:T(2,128)(2,1)} %get-tuple-element.883) | copy-start | bytes 4718596 | tf_op jit(solution)/shard_map/while
  43.0 2.1 copy-start.4
  74.1 7.9 %collective-permute-start = (bf16[24,4096]{1,0:T(8,128)(2,1)S(1)}, bf16[24,4096]{1,0:T(8,128)(2,1)S(1)}, u32[]{:S(2)}, u32[]{:S(2)}) collective-permute-start(bf16[24,4096]{1,0:T(8,128)(2,1)S(1)} %fusion.107), channel_id=1, source_target_pairs={{0,4},{4,8},{8,12},{1,5},{5,9},{9,13},{2,6},{6,10},{10,14},{3,7},{... | collective-permute-start | bytes 589832 | tf_op jit(solution)/shard_map/while/body/eval_jaxpr/ppermute | solution.py:16
  82.0 37.1 %all-gather.7.cloned.1.call-start = ((), (), s32[]{:S(2)}) async-start(), calls=%async_computation | async-start | bytes 1966080 | tf_op jit(solution)/shard_map/while/body/eval_jaxpr/all_gather | solution.py:131
  82.3 1.6 copy-start
  84.4 6.5 %copy-start.3 = (bf16[24,128,2,128]{3,2,1,0:T(2,128)(2,1)S(1)}, bf16[24,128,2,128]{3,2,1,0:T(2,128)(2,1)}, u32[]{:S(2)}) copy-start(bf16[24,128,2,128]{3,2,1,0:T(2,128)(2,1)} %get-tuple-element.883) | copy-start | bytes 4718596 | tf_op jit(solution)/shard_map/while
  90.2 2.1 copy-start.4
  120.8 7.9 %collective-permute-start = (bf16[24,4096]{1,0:T(8,128)(2,1)S(1)}, bf16[24,4096]{1,0:T(8,128)(2,1)S(1)}, u32[]{:S(2)}, u32[]{:S(2)}) collective-permute-start(bf16[24,4096]{1,0:T(8,128)(2,1)S(1)} %fusion.107), channel_id=1, source_target_pairs={{0,4},{4,8},{8,12},{1,5},{5,9},{9,13},{2,6},{6,10},{10,14},{3,7},{... | collective-permute-start | bytes 589832 | tf_op jit(solution)/shard_map/while/body/eval_jaxpr/ppermute | solution.py:16
  128.8 37.1 %all-gather.7.cloned.1.call-start = ((), (), s32[]{:S(2)}) async-start(), calls=%async_computation | async-start | bytes 1966080 | tf_op jit(solution)/shard_map/while/body/eval_jaxpr/all_gather | solution.py:131
  129.1 1.6 copy-start
  131.1 6.5 %copy-start.3 = (bf16[24,128,2,128]{3,2,1,0:T(2,128)(2,1)S(1)}, bf16[24,128,2,128]{3,2,1,0:T(2,128)(2,1)}, u32[]{:S(2)}) copy-start(bf16[24,128,2,128]{3,2,1,0:T(2,128)(2,1)} %get-tuple-element.883) | copy-start | bytes 4718596 | tf_op jit(solution)/shard_map/while
  136.9 2.1 copy-start.4
  167.6 7.9 %collective-permute-start = (bf16[24,4096]{1,0:T(8,128)(2,1)S(1)}, bf16[24,4096]{1,0:T(8,128)(2,1)S(1)}, u32[]{:S(2)}, u32[]{:S(2)}) collective-permute-start(bf16[24,4096]{1,0:T(8,128)(2,1)S(1)} %fusion.107), channel_id=1, source_target_pairs={{0,4},{4,8},{8,12},{1,5},{5,9},{9,13},{2,6},{6,10},{10,14},{3,7},{... | collective-permute-start | bytes 589832 | tf_op jit(solution)/shard_map/while/body/eval_jaxpr/ppermute | solution.py:16
  175.5 37.1 %all-gather.7.cloned.1.call-start = ((), (), s32[]{:S(2)}) async-start(), calls=%async_computation | async-start | bytes 1966080 | tf_op jit(solution)/shard_map/while/body/eval_jaxpr/all_gather | solution.py:131
  175.8 1.6 copy-start
  177.9 6.5 %copy-start.3 = (bf16[24,128,2,128]{3,2,1,0:T(2,128)(2,1)S(1)}, bf16[24,128,2,128]{3,2,1,0:T(2,128)(2,1)}, u32[]{:S(2)}) copy-start(bf16[24,128,2,128]{3,2,1,0:T(2,128)(2,1)} %get-tuple-element.883) | copy-start | bytes 4718596 | tf_op jit(solution)/shard_map/while
  183.7 2.1 copy-start.4
  214.3 7.9 %collective-permute-start = (bf16[24,4096]{1,0:T(8,128)(2,1)S(1)}, bf16[24,4096]{1,0:T(8,128)(2,1)S(1)}, u32[]{:S(2)}, u32[]{:S(2)}) collective-permute-start(bf16[24,4096]{1,0:T(8,128)(2,1)S(1)} %fusion.107), channel_id=1, source_target_pairs={{0,4},{4,8},{8,12},{1,5},{5,9},{9,13},{2,6},{6,10},{10,14},{3,7},{... | collective-permute-start | bytes 589832 | tf_op jit(solution)/shard_map/while/body/eval_jaxpr/ppermute | solution.py:16
  222.2 0.6 copy-start.5
  222.2 0.6 copy-start.6
  222.2 0.6 copy-start.7
Sparse Core Ops, SparseCore 0:
  51.3 21.1 all-gather.6
  98.5 20.6 all-gather.6
  145.2 20.6 all-gather.6
  191.9 20.6 all-gather.6
